TPU v7x, 256 devices: a whole 4x4x8 slice. The times are simulated.
256 devices in a mesh: grp: 4 (over z_lo, core), ctx: 16 (over z_hi, y), wid: 4 (over x).
Axes of the slice: x: 4, y: 4, z: 8 (z_hi: 4, z_lo: 2; z = z_hi * 2 + z_lo), core: 2. Of those that a mesh axis runs over, the one named last changes fastest.
Arguments:
- query: bfloat16 [256, 64, 128], P(None, 'wid'), may hold values from -64 to 64
- keys: bfloat16 [4, 4096, 8, 128], P(None, ('grp', 'ctx'), 'wid'), may hold values from -64 to 64
- values: bfloat16 [4, 4096, 8, 128], P(None, ('grp', 'ctx'), 'wid'), may hold values from -6 to 6
- lengths: int32 [4, 64], replicated, may hold values from 32 to 64
- query_pos: int32 [256], replicated, may hold values from 1024 to 4095
- resid: bfloat16 [256, 5120], P('wid', ('grp', 'ctx')), may hold values from -1.1953125 to 1.1953125
- out_weight: bfloat16 [8192, 5120], P('wid', ('grp', 'ctx')), may hold values from -0.0625 to 0.0625
- enc_weight: bfloat16 [5120, 24576], P('wid', ('grp', 'ctx')), may hold values from -0.078125 to 0.078125
- enc_bias: float32 [24576], P(('grp', 'ctx')), may hold values from -3 to 3
- dec_weight: bfloat16 [24576, 5120], P(('grp', 'ctx'), 'wid'), may hold values from -0.078125 to 0.078125
- dec_bias: float32 [5120], P('wid'), may hold values from -3 to 3
Outputs:
- layer_out: bfloat16 [256, 5120], P('wid', ('grp', 'ctx'))
- enc_grad: bfloat16 [5120, 24576], P('wid', ('grp', 'ctx'))
- enc_bias_grad: float32 [24576], P(('grp', 'ctx'))
- dec_grad: bfloat16 [24576, 5120], P(('grp', 'ctx'), 'wid')
- dec_bias_grad: float32 [5120], P('wid')
Inputs may be any that keep to these rules, and one draw needn't show every extreme that they name: `lengths`: live slots of a shard are its first ones.
All inputs are finite; a program needn't handle non-finite values.
Results may differ from a plain program's by a relative error of at most 0.024.
Values may be sent and summed in bfloat16 or wider, within the bound.
No kernel may reach another device: no remote copies, remote signals or barrier semaphores. Data moves between devices by JAX's collectives and lax.ppermute only.
A program may use at most 128 MiB of HBM per device.

v0:
```python
import jax
import jax.numpy as jnp
from jax import lax
from jax.sharding import Mesh
from jax.sharding import PartitionSpec as P

HD = 128
GRP_CTX = ("grp_0", "grp_1", "ctx_0", "ctx_1")


def combined_by_axis(shard, axes, combine):
    for axis in axes:
        pieces = jax.tree.map(
            lambda part, kind: lax.all_gather(part.astype(kind), axis),
            shard,
            (jnp.bfloat16, jnp.bfloat16, jnp.bfloat16),
        )
        widened = [
            jax.tree.map(lambda part, own: part[k].astype(own.dtype), pieces, shard)
            for k in range(lax.axis_size(axis))
        ]
        shard = widened[0]
        for theirs in widened[1:]:
            shard = combine(shard, theirs)
    return shard


def in_blocks(shard, dim, length):
    before, after = (shard.shape[:dim], shard.shape[dim + 1 :])
    return jnp.moveaxis(shard.reshape(*before, length, -1, *after), dim, 0)


def summed_on_arrival(shard, axis, dim):
    length = lax.axis_size(axis)
    blocks = lax.all_to_all(in_blocks(shard, dim, length), axis, 0, 0, tiled=True)
    return jnp.sum(blocks.astype(jnp.float32), axis=0)


def from_everyone(shard, axis):
    copies = jnp.broadcast_to(shard, (lax.axis_size(axis), *shard.shape))
    return lax.all_to_all(copies, axis, split_axis=0, concat_axis=0, tiled=True)


def taken_together(shard, axis):
    everything = from_everyone(shard, axis)
    return jnp.sum(everything.astype(jnp.float32), axis=0)


def sent_and_summed(shard, axis, dim):
    length = lax.axis_size(axis)
    blocks = lax.all_to_all(in_blocks(shard, dim, length), axis, 0, 0, tiled=True)
    return jnp.sum(blocks, axis=0)


def combine(earlier, later):
    peak_a, sum_a, weighted_a = earlier
    peak_b, sum_b, weighted_b = later
    peak = jnp.maximum(peak_a, peak_b)
    factor_a = jnp.exp(peak_a - peak)
    factor_b = jnp.exp(peak_b - peak)
    weight_sum = sum_a * factor_a + sum_b * factor_b
    weighted = weighted_a * factor_a[..., None] + weighted_b * factor_b[..., None]
    return (peak, weight_sum, weighted)


def body(
    query,
    keys,
    values,
    lengths,
    query_pos,
    resid,
    out_weight,
    enc_weight,
    enc_bias,
    dec_weight,
    dec_bias,
):
    seq_count, slot_count, kv_local, head_dim = keys.shape
    row_count = query.shape[0]
    heads_local = query.shape[1]
    group_size = heads_local // kv_local
    rows_each = row_count // seq_count
    shard_pos = lax.axis_index(GRP_CTX)
    shard_ids = jnp.arange(lengths.shape[1], dtype=jnp.int32)
    offset = jnp.sum(jnp.where(shard_ids[None, :] < shard_pos, lengths, 0), axis=1)
    live_count = jnp.sum(jnp.where(shard_ids[None, :] == shard_pos, lengths, 0), axis=1)
    slot_ids = jnp.arange(slot_count, dtype=jnp.int32)
    key_pos = offset[:, None] + slot_ids[None, :]
    live_slot = slot_ids[None, :] < live_count[:, None]
    row_position = query_pos.reshape(seq_count, rows_each)
    visible = live_slot[:, None, :] & (key_pos[:, None, :] <= row_position[:, :, None])
    visible_mask = visible[:, :, None, None, :]
    q_view = query.reshape(seq_count, rows_each, kv_local, group_size, head_dim)
    scores = jnp.einsum(
        "srkgd,sjkd->srkgj", q_view, keys, preferred_element_type=jnp.float32
    ) * HD ** (-0.5)
    local_peak = jnp.max(jnp.where(visible_mask, scores, -1e30), axis=-1)
    weights = jnp.where(visible_mask, jnp.exp(scores - local_peak[..., None]), 0.0)
    weight_sum = jnp.sum(weights, axis=-1)
    weights_low = weights.astype(jnp.bfloat16)
    weighted = jnp.einsum(
        "srkgj,sjkd->srkgd", weights_low, values, preferred_element_type=jnp.float32
    )
    weight_sum, weighted = (weight_sum, weighted)
    peak, weight_sum, weighted = combined_by_axis(
        (local_peak, weight_sum, weighted), GRP_CTX, combine
    )
    attention = (weighted / weight_sum[..., None]).astype(jnp.bfloat16)
    attention = attention.reshape(row_count, heads_local * head_dim)
    projected = jnp.dot(attention, out_weight, preferred_element_type=jnp.float32)
    mixed = summed_on_arrival(projected.astype(jnp.bfloat16), "wid", 0)
    layer_out = (mixed + resid.astype(jnp.float32)).astype(jnp.bfloat16)
    wide_rows = lax.all_gather(layer_out, GRP_CTX, axis=1, tiled=True)
    block = lax.all_to_all(wide_rows, "wid", split_axis=1, concat_axis=0, tiled=True)
    enc_part = jnp.dot(block, enc_weight, preferred_element_type=jnp.float32)
    preact = taken_together(enc_part.astype(jnp.bfloat16), "wid").astype(jnp.float32) + enc_bias
    latents = (jax.nn.softplus(4.0 * preact) * 0.25).astype(jnp.bfloat16)
    row_scale = row_count ** (-0.5)
    recon = sent_and_summed(
        jnp.dot(latents, dec_weight, preferred_element_type=jnp.float32), GRP_CTX, 0
    )
    piece_len = recon.shape[0]
    target = lax.dynamic_slice_in_dim(block, shard_pos * piece_len, piece_len, 0).astype(
        jnp.float32
    )
    scaled_error = ((recon + dec_bias - target) * row_scale).astype(jnp.bfloat16)
    error_all = lax.all_gather(scaled_error, GRP_CTX, axis=0, tiled=True)
    dec_bias_grad = jnp.sum(error_all, axis=0, dtype=jnp.float32)
    latent_part = lax.dot_general(
        error_all, dec_weight, (((1,), (1,)), ((), ())), preferred_element_type=jnp.float32
    )
    dec_grad = lax.dot_general(
        latents, error_all, (((0,), (0,)), ((), ())), preferred_element_type=jnp.float32
    )
    latent_grad = taken_together(latent_part.astype(jnp.bfloat16), "wid").astype(jnp.float32)
    preact_grad = (latent_grad * jax.nn.sigmoid(4.0 * preact)).astype(jnp.bfloat16)
    enc_grad = lax.dot_general(
        block, preact_grad, (((0,), (0,)), ((), ())), preferred_element_type=jnp.float32
    ).astype(jnp.bfloat16)
    enc_bias_grad = jnp.sum(preact_grad, axis=0, dtype=jnp.float32)
    return (layer_out, enc_grad, enc_bias_grad, dec_grad.astype(jnp.bfloat16), dec_bias_grad)


def solution(mesh):
    torus = Mesh(
        mesh.devices.reshape(2, 2, 4, 4, mesh.shape["wid"]),
        ("grp_0", "grp_1", "ctx_0", "ctx_1", "wid"),
    )
    in_specs = (
        P(None, "wid", None),
        P(None, GRP_CTX, "wid", None),
        P(None, GRP_CTX, "wid", None),
        P(),
        P(),
        P("wid", GRP_CTX),
        P("wid", GRP_CTX),
        P("wid", GRP_CTX),
        P(GRP_CTX),
        P(GRP_CTX, "wid"),
        P("wid"),
    )
    out_specs = (P("wid", GRP_CTX), P("wid", GRP_CTX), P(GRP_CTX), P(GRP_CTX, "wid"), P("wid"))
    return jax.shard_map(body, mesh=torus, in_specs=in_specs, out_specs=out_specs, check_vma=False)
```

profile of v0, /device:TPU:32, one launch (start us, length us, event | category | flops | bytes accessed | tf_op | source)
XLA Modules:
  0.0 675.0 jit_solution(17610328824982261202)
XLA Ops:
  7.3 0.9 select_reduce_fusion.1
  8.3 0.8 le.20
  9.2 2.0 fusion.2
  11.3 0.8 fusion.6
  12.0 0.7 copy.92
  12.8 0.4 fusion.7
  13.2 1.2 copy.94
  14.5 4.4 all-gather.1
  19.1 0.2 copy.96
  19.2 34.9 %all-gather.16.cloned.1.call-done = bf16[8,64,2,8,128]{4,3,2,1,0:T(8,128)(2,1)} async-done(((bf16[4,64,2,8,128]{4,3,2,1,0:T(8,128)(2,1)}), bf16[8,64,2,8,128]{4,3,2,1,0:T(8,128)(2,1)}) %all-gather.16.cloned.1.call-update) | async-done | bytes 2097168 | tf_op jit(solution)/shard_map/all_gather | solution.py:14
  54.1 3.9 fusion.1
  58.1 4.4 all-gather.2
  62.6 1.8 all_gather.60
  64.8 11.1 %all-gather.10.cloned.1.call-done = bf16[2,4,64,2,8,128]{5,4,3,2,1,0:T(8,128)(2,1)} async-done(((bf16[1,4,64,2,8,128]{5,4,3,2,1,0:T(8,128)(2,1)}), bf16[2,4,64,2,8,128]{5,4,3,2,1,0:T(8,128)(2,1)}) %all-gather.10.cloned.1.call-update) | async-done | bytes 2097168 | tf_op jit(solution)/shard_map/all_gather | solution.py:14
  75.9 4.0 add_convert_fusion.1
  79.9 1.8 all_gather.66
  81.8 15.0 %all_gather.62 = bf16[4,4,64,2,8]{2,4,3,1,0:T(8,128)(2,1)S(1)} all-gather(bf16[1,4,64,2,8]{2,4,3,1,0:T(8,128)(2,1)S(1)} %get-tuple-element.34), channel_id=1, replica_groups=mesh['grp_0'=2,'grp_1'=2,'ctx_0'=4,'ctx_1'=4,'wid'=4] {'ctx_0'}, dimensions={0}, use_global_device_ids=true | all-gather | bytes 40960 | tf_op jit(solution)/shard_map/all_gather | solution.py:14
  97.8 69.0 %all-gather.12.cloned.1.call-done = bf16[4,4,64,2,8,128]{5,4,3,2,1,0:T(8,128)(2,1)} async-done(((bf16[1,4,64,2,8,128]{5,4,3,2,1,0:T(8,128)(2,1)}), bf16[4,4,64,2,8,128]{5,4,3,2,1,0:T(8,128)(2,1)}) %all-gather.12.cloned.1.call-update) | async-done | bytes 4194320 | tf_op jit(solution)/shard_map/all_gather | solution.py:14
  166.8 7.6 %add_convert_fusion = bf16[1,4,64,2,8,128]{5,4,3,2,1,0:T(8,128)(2,1)} fusion(bf16[4,4,64,2,8,128]{5,4,3,2,1,0:T(8,128)(2,1)} %all-gather.12.cloned.1.call-done, f32[4,64,2,8]{3,2,1,0:T(2,128)S(1)} %copy.104, f32[4,64,2,8]{3,2,1,0:T(2,128)S(1)} %copy.103, f32[4,64,2,8]{3,2,1,0:T(2,128)S(1)} %copy.102, f32[4,64,2,8]{3,2,1,0:T(2,128)S(1)} %copy.101, ...), kind=kLoop, calls=%fused_computation.12 | loop fusion | flops 7340032 | bytes 5341184 | tf_op jit(solution)/shard_map/convert_element_type | solution.py:14
  174.5 13.7 %all_gather.67 = bf16[4,4,64,2,8]{2,4,3,1,0:T(8,128)(2,1)S(1)} all-gather(bf16[1,4,64,2,8]{2,4,3,1,0:T(8,128)(2,1)S(1)} %get-tuple-element.35), channel_id=1, replica_groups=mesh['grp_0'=2,'grp_1'=2,'ctx_0'=4,'ctx_1'=4,'wid'=4] {'ctx_0'}, dimensions={0}, use_global_device_ids=true | all-gather | bytes 40960 | tf_op jit(solution)/shard_map/all_gather | solution.py:14
  188.2 12.9 %all_gather.64 = bf16[4,4,64,2,8]{2,4,3,1,0:T(8,128)(2,1)S(1)} all-gather(bf16[1,4,64,2,8]{2,4,3,1,0:T(8,128)(2,1)S(1)} %get-tuple-element.28), channel_id=1, replica_groups=mesh['grp_0'=2,'grp_1'=2,'ctx_0'=4,'ctx_1'=4,'wid'=4] {'ctx_1'}, dimensions={0}, use_global_device_ids=true | all-gather | bytes 40960 | tf_op jit(solution)/shard_map/all_gather | solution.py:14
  201.0 12.2 %all_gather.68 = bf16[4,4,64,2,8]{2,4,3,1,0:T(8,128)(2,1)S(1)} all-gather(bf16[1,4,64,2,8]{2,4,3,1,0:T(8,128)(2,1)S(1)} %get-tuple-element.29), channel_id=1, replica_groups=mesh['grp_0'=2,'grp_1'=2,'ctx_0'=4,'ctx_1'=4,'wid'=4] {'ctx_1'}, dimensions={0}, use_global_device_ids=true | all-gather | bytes 40960 | tf_op jit(solution)/shard_map/all_gather | solution.py:14
  213.4 0.6 div.14
  214.1 1.5 div.15
  215.7 0.6 mul.304
  216.3 1.5 mul.305
  218.0 0.6 mul.307
  218.6 1.5 mul.308
  220.2 0.6 mul.310
  220.9 1.5 mul.311
  222.5 0.6 mul.313
  223.1 1.5 mul.314
  224.8 0.6 mul.316
  225.4 1.5 mul.317
  227.1 0.6 mul.319
  227.7 1.5 mul.320
  229.2 4.9 slice_convert_fusion.3
  234.2 2.7 reshape.388
  236.9 2.7 reshape.391
  239.6 2.7 reshape.393
  242.3 1.5 reshape.395
  243.8 9.3 %convolution_convert_fusion.5 = bf16[256,80]{0,1:T(8,128)(2,1)S(1)} fusion(bf16[2048,80]{0,1:T(8,128)(2,1)S(1)} %copy-done.4, f32[256,2048]{1,0:T(8,128)} %div.15, f32[256,2048]{1,0:T(8,128)} %reshape.395, f32[256,2048]{1,0:T(8,128)} %mul.320, f32[256,2048]{1,0:T(8,128)} %mul.317, f32[256,2048]{1,0:T(8,128)} %reshape.393, f32[256,2048]{1,0:T(8,128)} %mul.314, ...), kind=kOutput, calls=%fused_computation.24 | convolution fusion | flops 89673728 | bytes 23437312 | tf_op jit(solution)/shard_map/dot_general | solution.py:111
  253.2 9.8 %all_to_all.39 = bf16[4,64,80]{2,1,0:T(8,128)(2,1)S(1)} all-to-all(bf16[4,64,80]{2,1,0:T(8,128)(2,1)S(1)} %bitcast.336), channel_id=1, replica_groups=mesh['grp_0'=2,'grp_1'=2,'ctx_0'=4,'ctx_1'=4,'wid'=4] {'wid'}, dimensions={0} | all-to-all | bytes 81920 | tf_op jit(solution)/shard_map/all_to_all | solution.py:35
  263.0 158.3 %all-gather.3 = bf16[64,80,64]{1,2,0:T(8,128)(2,1)S(1)} all-gather(bf16[1,80,64]{1,2,0:T(8,128)(2,1)S(1)} %bitcast.339), channel_id=1, replica_groups=mesh['grp_0'=2,'grp_1'=2,'ctx_0'=4,'ctx_1'=4,'wid'=4] {'grp_0','grp_1','..., dimensions={0}, use_global_device_ids=true | all-gather | bytes 665600 | tf_op jit(solution)/shard_map/all_gather | solution.py:114
  421.4 0.7 copy.113
  422.1 2.1 reshape.418
  424.2 13.2 %all_to_all.40 = bf16[64,4,1280]{2,0,1:T(8,128)(2,1)S(1)} all-to-all(bf16[64,4,1280]{2,0,1:T(8,128)(2,1)S(1)} %bitcast.335), channel_id=1, replica_groups=mesh['grp_0'=2,'grp_1'=2,'ctx_0'=4,'ctx_1'=4,'wid'=4] {'wid'}, dimensions={1} | all-to-all | bytes 1310720 | tf_op jit(solution)/shard_map/all_to_all | solution.py:115
  437.4 0.5 convolution_convert_fusion.4
  438.1 12.0 %all_to_all.41 = bf16[4,256,384]{2,1,0:T(8,128)(2,1)S(1)} all-to-all(bf16[4,256,384]{2,1,0:T(8,128)(2,1)S(1)} %broadcast_in_dim.46), channel_id=1, replica_groups=mesh['grp_0'=2,'grp_1'=2,'ctx_0'=4,'ctx_1'=4,'wid'=4] {'wid'}, dimensions={0} | all-to-all | bytes 1572864 | tf_op jit(solution)/shard_map/all_to_all | solution.py:41
  450.2 0.7 fusion.80
  450.9 1.5 reshape.379
  452.4 6.4 all-to-all-start.3
  458.7 33.8 %all-to-all-done.3 = f32[64,4,1280]{2,1,0:T(4,128)S(1)} async-done(((f32[64,4,1280]{2,1,0:T(4,128)}), f32[64,4,1280]{2,1,0:T(4,128)S(1)}, u32[]{:S(2)}, u32[]{:S(2)}) %all-to-all-start.3) | async-done | bytes 1310752 | tf_op jit(solution)/shard_map/all_to_all | solution.py:51
  492.6 0.2 reduce_sum.86
  492.8 156.8 %all-gather.4 = bf16[64,4,1280]{2,1,0:T(4,128)(2,1)S(1)} all-gather(bf16[1,4,1280]{2,1,0:T(4,128)(2,1)S(1)} %fusion.78), channel_id=1, replica_groups=mesh['grp_0'=2,'grp_1'=2,'ctx_0'=4,'ctx_1'=4,'wid'=4] {'grp_0','grp_1','..., dimensions={0}, use_global_device_ids=true | all-gather | bytes 665600 | tf_op jit(solution)/shard_map/all_gather | solution.py:128
  649.8 0.5 convolution_convert_fusion.3
  650.3 0.9 broadcast_in_dim.78
  651.3 4.2 all-to-all-start.4
  655.5 0.7 convert_reduce_fusion.2
  656.2 1.6 convolution_convert_fusion
  657.8 7.2 %all-to-all-done.4 = bf16[4,256,384]{2,1,0:T(8,128)(2,1)} async-done(((bf16[4,256,384]{2,1,0:T(8,128)(2,1)}), bf16[4,256,384]{2,1,0:T(8,128)(2,1)}, u32[]{:S(2)}, u32[]{:S(2)}) %all-to-all-start.4) | async-done | bytes 786464 | tf_op jit(solution)/shard_map/all_to_all | solution.py:41
  665.0 1.3 convert_reduce_fusion
  666.3 0.7 convert_reduce_fusion.3
  667.0 1.5 convolution_convert_fusion.1
  (65 shorter events, 3.8 us)
Async XLA Ops:
  7.2 2.0 copy-start
  7.2 46.9 %all-gather.16.cloned.1.call-start = ((), (), s32[]{:S(2)}) async-start(), calls=%async_computation.8 | async-start | bytes 3145728 | tf_op jit(solution)/shard_map/all_gather | solution.py:14
  11.3 1.5 copy-start.5
  14.4 61.5 %all-gather.10.cloned.1.call-start = ((), (), s32[]{:S(2)}) async-start(), calls=%async_computation.5 | async-start | bytes 3145728 | tf_op jit(solution)/shard_map/all_gather | solution.py:14
  58.1 108.7 %all-gather.12.cloned.1.call-start = ((), (), s32[]{:S(2)}) async-start(), calls=%async_computation.6 | async-start | bytes 5242880 | tf_op jit(solution)/shard_map/all_gather | solution.py:14
  79.9 149.4 %all-gather.14.cloned.1.call-start = ((), (), s32[]{:S(2)}) async-start(), calls=%async_computation.7 | async-start | bytes 5242880 | tf_op jit(solution)/shard_map/all_gather | solution.py:14
  242.3 1.5 copy-start.4
  243.8 19.2 %copy-start.7 = (bf16[64,80]{1,0:T(8,128)(2,1)S(1)}, bf16[64,80]{1,0:T(8,128)(2,1)}, u32[]{:S(2)}) copy-start(bf16[64,80]{1,0:T(8,128)(2,1)} %param.16) | copy-start | bytes 30724
  263.0 161.1 %copy-start.6 = (bf16[64,80]{1,0:T(8,128)(2,1)}, bf16[64,80]{1,0:T(8,128)(2,1)S(1)}, u32[]{:S(2)}) copy-start(bf16[64,80]{1,0:T(8,128)(2,1)S(1)} %add_convert_fusion.2) | copy-start | bytes 30724
  422.0 15.4 %copy-start.3 = (bf16[1280,384]{1,0:T(8,128)(2,1)S(1)}, bf16[1280,384]{1,0:T(8,128)(2,1)}, u32[]{:S(2)}) copy-start(bf16[1280,384]{1,0:T(8,128)(2,1)} %param.18) | copy-start | bytes 2949124
  438.0 12.2 %copy-start.2 = (bf16[384,1280]{1,0:T(8,128)(2,1)S(1)}, bf16[384,1280]{1,0:T(8,128)(2,1)}, u32[]{:S(2)}) copy-start(bf16[384,1280]{1,0:T(8,128)(2,1)} %param.20) | copy-start | bytes 2949124
  438.0 12.2 %copy-start.8 = (f32[384]{0:T(512)S(1)}, f32[384]{0:T(512)}, u32[]{:S(2)}) copy-start(f32[384]{0:T(512)} %param.19) | copy-start | bytes 4612
  452.4 40.4 %copy-start.9 = (f32[1280]{0:T(1024)S(1)}, f32[1280]{0:T(1024)}, u32[]{:S(2)}) copy-start(f32[1280]{0:T(1024)} %param.21) | copy-start | bytes 15364
  452.4 40.2 %all-to-all-start.3 = ((f32[64,4,1280]{2,1,0:T(4,128)}), f32[64,4,1280]{2,1,0:T(4,128)S(1)}, u32[]{:S(2)}, u32[]{:S(2)}) async-start(f32[64,4,1280]{2,1,0:T(4,128)} %reshape.379), calls=%async_computation.3 | async-start | bytes 2621440 | tf_op jit(solution)/shard_map/all_to_all | solution.py:51
  651.3 13.7 %all-to-all-start.4 = ((bf16[4,256,384]{2,1,0:T(8,128)(2,1)}), bf16[4,256,384]{2,1,0:T(8,128)(2,1)}, u32[]{:S(2)}, u32[]{:S(2)}) async-start(bf16[4,256,384]{2,1,0:T(8,128)(2,1)} %broadcast_in_dim.78), calls=%async_computation.4 | async-start | bytes 1572864 | tf_op jit(solution)/shard_map/all_to_all | solution.py:41
  656.2 12.3 %copy-start.1 = (bf16[256,16,128]{2,1,0:T(8,128)(2,1)S(1)}, bf16[256,16,128]{2,1,0:T(8,128)(2,1)}, u32[]{:S(2)}) copy-start(bf16[256,16,128]{2,1,0:T(8,128)(2,1)} %param.11) | copy-start | bytes 3145732
Sparse Core Ops, SparseCore 0:
  14.5 39.5 all-gather.15
  58.2 17.6 all-gather.9
  80.0 86.7 all-gather.11
  174.6 51.0 all-gather.13
where the time goes:
time: 676 us; the launch traced here: 675 us
  blocking collectives  416 us (62%)
  waiting for transfers between devices  156 us (23%)
  local copies, waits for them, and re-layouts  35.3 us (5%)
  other arithmetic  25.7 us (4%)
  matrix products  16.5 us (2%)
  between operations  14.2 us (2%)
  starting transfers between devices  10.7 us (2%)
    all_gather x1, blocking collectives, body(): wide_rows = lax.all_gather(layer_out, GRP_CTX, axis=1, tiled=True)  158 us
    all_gather x1, blocking collectives, body(): error_all = lax.all_gather(scaled_error, GRP_CTX, axis=0, tiled=True)  157 us
    all_gather x4, waiting for transfers between devices, combined_by_axis(): lax.all_gather(part.astype(kind), axis)  115 us
    all_gather x8, blocking collectives, combined_by_axis(): lax.all_gather(part.astype(kind), axis)  66.3 us
    all_to_all x1, waiting for transfers between devices, sent_and_summed(): lax.all_to_all(in_blocks(shard, dim, length), axis, 0, 0, tiled=True)  33.8 us
    convert_element_type x7, other arithmetic, combined_by_axis(): part.astype(kind)  15.6 us
  transfers between devices with their start and end apart: 6, of which 5 were waited for; matrix products, arithmetic and copies ran while one was open for 3% of the time, Pallas kernels for 0%

commit v1 on v0

--- a/solution.py
+++ b/solution.py
@@ -111,7 +111,9 @@
     projected = jnp.dot(attention, out_weight, preferred_element_type=jnp.float32)
     mixed = summed_on_arrival(projected.astype(jnp.bfloat16), "wid", 0)
     layer_out = (mixed + resid.astype(jnp.float32)).astype(jnp.bfloat16)
-    wide_rows = lax.all_gather(layer_out, GRP_CTX, axis=1, tiled=True)
+    wide_rows = jnp.concatenate(
+        lax.all_to_all(jnp.stack([layer_out] * lax.axis_size(GRP_CTX)), GRP_CTX, 0, 0), axis=1
+    )
     block = lax.all_to_all(wide_rows, "wid", split_axis=1, concat_axis=0, tiled=True)
     enc_part = jnp.dot(block, enc_weight, preferred_element_type=jnp.float32)
     preact = taken_together(enc_part.astype(jnp.bfloat16), "wid").astype(jnp.float32) + enc_bias

time: 676 us -> 556 us (0.82)
  blocking collectives: 416 us -> 297 us
    all_gather x1 -> x0, blocking collectives: 158 us -> none  [body(): wide_rows = lax.all_gather(layer_out, GRP_CTX, axis=1, tiled=True)]
    all_to_all x0 -> x1, blocking collectives: none -> 35.4 us  [body(): lax.all_to_all(jnp.stack([layer_out] * lax.axis_size(GRP_CTX)), GRP_CTX,...]
  transfers between devices with their start and end apart: 6 -> 6, of which waited for: 5 -> 5; matrix products, arithmetic and copies ran while one was open for 3% -> 4% of each run, Pallas kernels for 0% -> 0%
where the time goes in v1:
time: 556 us; the launch traced here: 555 us
  blocking collectives  297 us (53%)
  waiting for transfers between devices  156 us (28%)
  local copies, waits for them, and re-layouts  34.8 us (6%)
  other arithmetic  25.7 us (5%)
  matrix products  16.5 us (3%)
  between operations  14.2 us (3%)
  starting transfers between devices  10.4 us (2%)
    all_gather x1, blocking collectives, body(): error_all = lax.all_gather(scaled_error, GRP_CTX, axis=0, tiled=True)  157 us
    all_gather x4, waiting for transfers between devices, combined_by_axis(): lax.all_gather(part.astype(kind), axis)  115 us
    all_gather x8, blocking collectives, combined_by_axis(): lax.all_gather(part.astype(kind), axis)  66.3 us
    all_to_all x1, blocking collectives, body(): lax.all_to_all(jnp.stack([layer_out] * lax.axis_size(GRP_CTX)), GRP_CTX,...  35.4 us
    all_to_all x1, waiting for transfers between devices, sent_and_summed(): lax.all_to_all(in_blocks(shard, dim, length), axis, 0, 0, tiled=True)  33.8 us
    convert_element_type x7, other arithmetic, combined_by_axis(): part.astype(kind)  15.6 us
    all_to_all x1, blocking collectives, from_everyone(): return lax.all_to_all(copies, axis, split_axis=0, concat_axis=0, tiled=True)  14.7 us
    all_to_all x1, blocking collectives, body(): lax.all_to_all(wide_rows, 'wid', split_axis=1, concat_axis=0, tiled=True)  13.9 us
  transfers between devices with their start and end apart: 6, of which 5 were waited for; matrix products, arithmetic and copies ran while one was open for 4% of the time, Pallas kernels for 0%

profile of v1, /device:TPU:32, one launch (start us, length us, event | category | flops | bytes accessed | tf_op | source)
XLA Modules:
  0.0 554.7 jit_solution(16289684685825562323)
XLA Ops:
  7.3 0.9 select_reduce_fusion.1
  8.3 0.8 le.20
  9.2 2.0 fusion.2
  11.3 0.8 fusion.6
  12.0 0.7 copy.91
  12.8 0.4 fusion.7
  13.2 1.2 copy.93
  14.5 4.4 all-gather.1
  19.2 34.9 %all-gather.15.cloned.1.call-done = bf16[8,64,2,8,128]{4,3,2,1,0:T(8,128)(2,1)} async-done(((bf16[4,64,2,8,128]{4,3,2,1,0:T(8,128)(2,1)}), bf16[8,64,2,8,128]{4,3,2,1,0:T(8,128)(2,1)}) %all-gather.15.cloned.1.call-update) | async-done | bytes 2097168 | tf_op jit(solution)/shard_map/all_gather | solution.py:14
  54.1 3.9 fusion.1
  58.1 4.4 all-gather.2
  62.6 1.8 all_gather.57
  64.8 11.1 %all-gather.9.cloned.1.call-done = bf16[2,4,64,2,8,128]{5,4,3,2,1,0:T(8,128)(2,1)} async-done(((bf16[1,4,64,2,8,128]{5,4,3,2,1,0:T(8,128)(2,1)}), bf16[2,4,64,2,8,128]{5,4,3,2,1,0:T(8,128)(2,1)}) %all-gather.9.cloned.1.call-update) | async-done | bytes 2097168 | tf_op jit(solution)/shard_map/all_gather | solution.py:14
  75.9 4.0 add_convert_fusion.1
  79.9 1.8 all_gather.63
  81.8 15.0 %all_gather.59 = bf16[4,4,64,2,8]{2,4,3,1,0:T(8,128)(2,1)S(1)} all-gather(bf16[1,4,64,2,8]{2,4,3,1,0:T(8,128)(2,1)S(1)} %get-tuple-element.34), channel_id=1, replica_groups=mesh['grp_0'=2,'grp_1'=2,'ctx_0'=4,'ctx_1'=4,'wid'=4] {'ctx_0'}, dimensions={0}, use_global_device_ids=true | all-gather | bytes 40960 | tf_op jit(solution)/shard_map/all_gather | solution.py:14
  97.8 69.0 %all-gather.11.cloned.1.call-done = bf16[4,4,64,2,8,128]{5,4,3,2,1,0:T(8,128)(2,1)} async-done(((bf16[1,4,64,2,8,128]{5,4,3,2,1,0:T(8,128)(2,1)}), bf16[4,4,64,2,8,128]{5,4,3,2,1,0:T(8,128)(2,1)}) %all-gather.11.cloned.1.call-update) | async-done | bytes 4194320 | tf_op jit(solution)/shard_map/all_gather | solution.py:14
  166.8 7.6 %add_convert_fusion = bf16[1,4,64,2,8,128]{5,4,3,2,1,0:T(8,128)(2,1)} fusion(bf16[4,4,64,2,8,128]{5,4,3,2,1,0:T(8,128)(2,1)} %all-gather.11.cloned.1.call-done, f32[4,64,2,8]{3,2,1,0:T(2,128)S(1)} %copy.103, f32[4,64,2,8]{3,2,1,0:T(2,128)S(1)} %copy.102, f32[4,64,2,8]{3,2,1,0:T(2,128)S(1)} %copy.101, f32[4,64,2,8]{3,2,1,0:T(2,128)S(1)} %copy.100, ...), kind=kLoop, calls=%fused_computation.12 | loop fusion | flops 7340032 | bytes 5341184 | tf_op jit(solution)/shard_map/convert_element_type | solution.py:14
  174.5 13.7 %all_gather.64 = bf16[4,4,64,2,8]{2,4,3,1,0:T(8,128)(2,1)S(1)} all-gather(bf16[1,4,64,2,8]{2,4,3,1,0:T(8,128)(2,1)S(1)} %get-tuple-element.35), channel_id=1, replica_groups=mesh['grp_0'=2,'grp_1'=2,'ctx_0'=4,'ctx_1'=4,'wid'=4] {'ctx_0'}, dimensions={0}, use_global_device_ids=true | all-gather | bytes 40960 | tf_op jit(solution)/shard_map/all_gather | solution.py:14
  188.2 12.9 %all_gather.61 = bf16[4,4,64,2,8]{2,4,3,1,0:T(8,128)(2,1)S(1)} all-gather(bf16[1,4,64,2,8]{2,4,3,1,0:T(8,128)(2,1)S(1)} %get-tuple-element.28), channel_id=1, replica_groups=mesh['grp_0'=2,'grp_1'=2,'ctx_0'=4,'ctx_1'=4,'wid'=4] {'ctx_1'}, dimensions={0}, use_global_device_ids=true | all-gather | bytes 40960 | tf_op jit(solution)/shard_map/all_gather | solution.py:14
  201.0 12.2 %all_gather.65 = bf16[4,4,64,2,8]{2,4,3,1,0:T(8,128)(2,1)S(1)} all-gather(bf16[1,4,64,2,8]{2,4,3,1,0:T(8,128)(2,1)S(1)} %get-tuple-element.29), channel_id=1, replica_groups=mesh['grp_0'=2,'grp_1'=2,'ctx_0'=4,'ctx_1'=4,'wid'=4] {'ctx_1'}, dimensions={0}, use_global_device_ids=true | all-gather | bytes 40960 | tf_op jit(solution)/shard_map/all_gather | solution.py:14
  213.4 0.6 div.14
  214.1 1.5 div.15
  215.7 0.6 mul.304
  216.3 1.5 mul.305
  218.0 0.6 mul.307
  218.6 1.5 mul.308
  220.2 0.6 mul.310
  220.9 1.5 mul.311
  222.5 0.6 mul.313
  223.1 1.5 mul.314
  224.8 0.6 mul.316
  225.4 1.5 mul.317
  227.1 0.6 mul.319
  227.7 1.5 mul.320
  229.2 4.9 slice_convert_fusion.3
  234.2 2.7 reshape.396
  236.9 2.7 reshape.399
  239.6 2.7 reshape.401
  242.3 1.5 reshape.403
  243.8 9.3 %convolution_convert_fusion.5 = bf16[256,80]{0,1:T(8,128)(2,1)S(1)} fusion(bf16[2048,80]{0,1:T(8,128)(2,1)S(1)} %copy-done.4, f32[256,2048]{1,0:T(8,128)} %div.15, f32[256,2048]{1,0:T(8,128)} %reshape.403, f32[256,2048]{1,0:T(8,128)} %mul.320, f32[256,2048]{1,0:T(8,128)} %mul.317, f32[256,2048]{1,0:T(8,128)} %reshape.401, f32[256,2048]{1,0:T(8,128)} %mul.314, ...), kind=kOutput, calls=%fused_computation.24 | convolution fusion | flops 89673728 | bytes 23437312 | tf_op jit(solution)/shard_map/dot_general | solution.py:111
  253.2 9.8 %all_to_all.44 = bf16[4,64,80]{2,1,0:T(8,128)(2,1)S(1)} all-to-all(bf16[4,64,80]{2,1,0:T(8,128)(2,1)S(1)} %bitcast.326), channel_id=1, replica_groups=mesh['grp_0'=2,'grp_1'=2,'ctx_0'=4,'ctx_1'=4,'wid'=4] {'wid'}, dimensions={0} | all-to-all | bytes 81920 | tf_op jit(solution)/shard_map/all_to_all | solution.py:35
  263.0 0.2 stack.2
  263.3 35.4 %all_to_all.45 = bf16[64,64,80]{2,1,0:T(8,128)(2,1)S(1)} all-to-all(bf16[64,64,80]{2,1,0:T(8,128)(2,1)S(1)} %stack.2), channel_id=1, replica_groups=mesh['grp_0'=2,'grp_1'=2,'ctx_0'=4,'ctx_1'=4,'wid'=4] {'grp_0','grp_1','..., dimensions={0} | all-to-all | bytes 1310720 | tf_op jit(solution)/shard_map/all_to_all | solution.py:115
  298.7 0.7 copy.112
  299.4 1.3 all_to_all.31
  300.8 13.9 %all_to_all.46 = bf16[64,4,1280]{2,0,1:T(8,128)(2,1)S(1)} all-to-all(bf16[64,4,1280]{2,0,1:T(8,128)(2,1)S(1)} %copy.113), channel_id=1, replica_groups=mesh['grp_0'=2,'grp_1'=2,'ctx_0'=4,'ctx_1'=4,'wid'=4] {'wid'}, dimensions={1} | all-to-all | bytes 1310720 | tf_op jit(solution)/shard_map/all_to_all | solution.py:117
  314.8 0.5 convolution_convert_fusion.4
  315.4 14.7 %all_to_all.47 = bf16[4,256,384]{2,1,0:T(8,128)(2,1)S(1)} all-to-all(bf16[4,256,384]{2,1,0:T(8,128)(2,1)S(1)} %broadcast_in_dim.46), channel_id=1, replica_groups=mesh['grp_0'=2,'grp_1'=2,'ctx_0'=4,'ctx_1'=4,'wid'=4] {'wid'}, dimensions={0} | all-to-all | bytes 1572864 | tf_op jit(solution)/shard_map/all_to_all | solution.py:41
  330.2 0.7 fusion.80
  330.8 1.5 reshape.387
  332.3 6.1 %all-to-all-start.4 = ((f32[64,4,1280]{2,1,0:T(4,128)}), f32[64,4,1280]{2,1,0:T(4,128)S(1)}, u32[]{:S(2)}, u32[]{:S(2)}) async-start(f32[64,4,1280]{2,1,0:T(4,128)} %reshape.387), calls=%async_computation.4 | async-start | bytes 2621440 | tf_op jit(solution)/shard_map/all_to_all | solution.py:51
  338.4 33.8 %all-to-all-done.4 = f32[64,4,1280]{2,1,0:T(4,128)S(1)} async-done(((f32[64,4,1280]{2,1,0:T(4,128)}), f32[64,4,1280]{2,1,0:T(4,128)S(1)}, u32[]{:S(2)}, u32[]{:S(2)}) %all-to-all-start.4) | async-done | bytes 1310752 | tf_op jit(solution)/shard_map/all_to_all | solution.py:51
  372.2 0.2 reduce_sum.86
  372.5 156.8 %all-gather.3 = bf16[64,4,1280]{2,1,0:T(4,128)(2,1)S(1)} all-gather(bf16[1,4,1280]{2,1,0:T(4,128)(2,1)S(1)} %fusion.78), channel_id=1, replica_groups=mesh['grp_0'=2,'grp_1'=2,'ctx_0'=4,'ctx_1'=4,'wid'=4] {'grp_0','grp_1','..., dimensions={0}, use_global_device_ids=true | all-gather | bytes 665600 | tf_op jit(solution)/shard_map/all_gather | solution.py:130
  529.5 0.5 convolution_convert_fusion.3
  530.0 0.9 broadcast_in_dim.78
  530.9 4.2 all-to-all-start.5
  535.1 0.7 convert_reduce_fusion.2
  535.8 1.6 convolution_convert_fusion
  537.4 7.2 %all-to-all-done.5 = bf16[4,256,384]{2,1,0:T(8,128)(2,1)} async-done(((bf16[4,256,384]{2,1,0:T(8,128)(2,1)}), bf16[4,256,384]{2,1,0:T(8,128)(2,1)}, u32[]{:S(2)}, u32[]{:S(2)}) %all-to-all-start.5) | async-done | bytes 786464 | tf_op jit(solution)/shard_map/all_to_all | solution.py:41
  544.7 1.3 convert_reduce_fusion
  546.0 0.7 convert_reduce_fusion.3
  546.7 1.5 convolution_convert_fusion.1
  (66 shorter events, 4.0 us)
Async XLA Ops:
  7.2 2.0 copy-start
  7.2 46.9 %all-gather.15.cloned.1.call-start = ((), (), s32[]{:S(2)}) async-start(), calls=%async_computation.9 | async-start | bytes 3145728 | tf_op jit(solution)/shard_map/all_gather | solution.py:14
  11.3 1.5 copy-start.5
  14.4 61.5 %all-gather.9.cloned.1.call-start = ((), (), s32[]{:S(2)}) async-start(), calls=%async_computation.6 | async-start | bytes 3145728 | tf_op jit(solution)/shard_map/all_gather | solution.py:14
  58.1 108.7 %all-gather.11.cloned.1.call-start = ((), (), s32[]{:S(2)}) async-start(), calls=%async_computation.7 | async-start | bytes 5242880 | tf_op jit(solution)/shard_map/all_gather | solution.py:14
  79.9 149.4 %all-gather.13.cloned.1.call-start = ((), (), s32[]{:S(2)}) async-start(), calls=%async_computation.8 | async-start | bytes 5242880 | tf_op jit(solution)/shard_map/all_gather | solution.py:14
  242.3 1.5 copy-start.4
  243.8 19.2 %copy-start.7 = (bf16[64,80]{1,0:T(8,128)(2,1)S(1)}, bf16[64,80]{1,0:T(8,128)(2,1)}, u32[]{:S(2)}) copy-start(bf16[64,80]{1,0:T(8,128)(2,1)} %param.16) | copy-start | bytes 30724
  263.0 36.4 %copy-start.6 = (bf16[64,80]{1,0:T(8,128)(2,1)}, bf16[64,80]{1,0:T(8,128)(2,1)S(1)}, u32[]{:S(2)}) copy-start(bf16[64,80]{1,0:T(8,128)(2,1)S(1)} %add_convert_fusion.2) | copy-start | bytes 30724
  299.4 15.3 %copy-start.3 = (bf16[1280,384]{1,0:T(8,128)(2,1)S(1)}, bf16[1280,384]{1,0:T(8,128)(2,1)}, u32[]{:S(2)}) copy-start(bf16[1280,384]{1,0:T(8,128)(2,1)} %param.18) | copy-start | bytes 2949124
  315.3 14.9 %copy-start.2 = (bf16[384,1280]{1,0:T(8,128)(2,1)S(1)}, bf16[384,1280]{1,0:T(8,128)(2,1)}, u32[]{:S(2)}) copy-start(bf16[384,1280]{1,0:T(8,128)(2,1)} %param.20) | copy-start | bytes 2949124
  315.3 14.9 %copy-start.8 = (f32[384]{0:T(512)S(1)}, f32[384]{0:T(512)}, u32[]{:S(2)}) copy-start(f32[384]{0:T(512)} %param.19) | copy-start | bytes 4612
  332.3 40.2 %copy-start.9 = (f32[1280]{0:T(1024)S(1)}, f32[1280]{0:T(1024)}, u32[]{:S(2)}) copy-start(f32[1280]{0:T(1024)} %param.21) | copy-start | bytes 15364
  332.3 39.9 %all-to-all-start.4 = ((f32[64,4,1280]{2,1,0:T(4,128)}), f32[64,4,1280]{2,1,0:T(4,128)S(1)}, u32[]{:S(2)}, u32[]{:S(2)}) async-start(f32[64,4,1280]{2,1,0:T(4,128)} %reshape.387), calls=%async_computation.4 | async-start | bytes 2621440 | tf_op jit(solution)/shard_map/all_to_all | solution.py:51
  530.9 13.7 %all-to-all-start.5 = ((bf16[4,256,384]{2,1,0:T(8,128)(2,1)}), bf16[4,256,384]{2,1,0:T(8,128)(2,1)}, u32[]{:S(2)}, u32[]{:S(2)}) async-start(bf16[4,256,384]{2,1,0:T(8,128)(2,1)} %broadcast_in_dim.78), calls=%async_computation.5 | async-start | bytes 1572864 | tf_op jit(solution)/shard_map/all_to_all | solution.py:41
  535.8 12.3 %copy-start.1 = (bf16[256,16,128]{2,1,0:T(8,128)(2,1)S(1)}, bf16[256,16,128]{2,1,0:T(8,128)(2,1)}, u32[]{:S(2)}) copy-start(bf16[256,16,128]{2,1,0:T(8,128)(2,1)} %param.11) | copy-start | bytes 3145732
Sparse Core Ops, SparseCore 0:
  14.5 39.5 all-gather.14
  58.2 17.6 all-gather.8
  80.0 86.7 all-gather.10
  174.6 51.0 all-gather.12
